TPU v7x, 32 devices: a whole 2x2x4 slice. The times are simulated.
32 devices in a mesh: section: 4 (over y, x), tok: 4 (over z), head: 2 (over core).
Axes of the slice: x: 2, y: 2, z: 4, core: 2. Of those that a mesh axis runs over, the one named last changes fastest.
Arguments:
- group_in: bfloat16 [4, 512, 2048], P('section', 'tok'), may hold values from -6 to 6
- w_qkv: bfloat16 [4, 3, 2048, 2048], P('section', None, 'tok', 'head'), may hold values from -0.125 to 0.125
- w_out: bfloat16 [4, 2048, 2048], P('section', 'head', 'tok'), may hold values from -0.125 to 0.125
- step_sizes: float32 [4, 512, 4], P('section', 'tok', 'head'), may hold values from 0.05 to 1
- fast_weights: bfloat16 [4, 4, 3, 512, 512], P('section', 'head'), may hold values from -0.25 to 0.25
- momentum: bfloat16 [4, 4, 3, 512, 512], P('section', 'head'), may hold values from -16 to 16
- momentum_decay: float32 [4, 4], P('section', 'head'), may hold values from 0.5 to 0.95
- fast_rate: float32 [4, 4], P('section', 'head'), may hold values from 0.3 to 1
Outputs:
- handed: bfloat16 [4, 512, 2048], P('section', 'tok', 'head')
- fast_next: bfloat16 [4, 4, 3, 512, 512], P('section', 'head')
All inputs are finite; a program needn't handle non-finite values.
Results may differ from a plain program's by a relative error of at most 0.015.
Values may be sent and summed in bfloat16 or wider, within the bound.
A program may use at most 128 MiB of HBM per device.

v0:
```python
import jax
import jax.numpy as jnp
from jax import lax
from jax.sharding import PartitionSpec as P

NS_ITERS = 2
coef_linear = 3.4445
coef_cubic = -4.775
coef_quintic = 2.0315


def passed_along(value, axis, steps):
    count = lax.axis_size(axis)
    pairs = [(source, (source + steps) % count) for source in range(count)]
    return lax.ppermute(value, axis, pairs)


def rms_rows(values_in, epsilon):
    return values_in * lax.rsqrt(jnp.mean(values_in * values_in, axis=-1, keepdims=True) + epsilon)


def fast_grads(key_rows, value_rows, step_rates, weights):
    gate_pre = jnp.einsum(
        "thi,hij->thj", key_rows, weights[:, 0], preferred_element_type=jnp.float32
    )
    up_pre = jnp.einsum("thi,hij->thj", key_rows, weights[:, 1], preferred_element_type=jnp.float32)
    squash = jax.nn.sigmoid(gate_pre)
    hidden = (gate_pre * squash * up_pre).astype(jnp.bfloat16)
    errors = (-(step_rates[:, :, None] * value_rows.astype(jnp.float32))).astype(jnp.bfloat16)
    back_hidden = jnp.einsum(
        "thi,hij->thj", errors, weights[:, 2], preferred_element_type=jnp.float32
    )
    grad_gate = (back_hidden * up_pre * squash * (1.0 + gate_pre * (1.0 - squash))).astype(
        jnp.bfloat16
    )
    grad_up = (back_hidden * gate_pre * squash).astype(jnp.bfloat16)
    grad_first = jnp.einsum("thi,thj->hij", key_rows, grad_gate, preferred_element_type=jnp.float32)
    grad_third = jnp.einsum("thi,thj->hij", key_rows, grad_up, preferred_element_type=jnp.float32)
    grad_second = jnp.einsum("thi,thj->hij", errors, hidden, preferred_element_type=jnp.float32)
    return jnp.stack([grad_first, grad_third, grad_second], axis=1)


def newton_step(rows_in, gathered):
    gram_matrix = jnp.einsum(
        "mij,mik->mjk", gathered, gathered, preferred_element_type=jnp.float32
    ).astype(jnp.bfloat16)
    cubic_term = jnp.einsum(
        "mij,mjk->mik", rows_in, gram_matrix, preferred_element_type=jnp.float32
    )
    quintic_term = jnp.einsum(
        "mij,mjk->mik",
        cubic_term.astype(jnp.bfloat16),
        gram_matrix,
        preferred_element_type=jnp.float32,
    )
    return (
        coef_linear * rows_in.astype(jnp.float32)
        + coef_cubic * cubic_term
        + coef_quintic * quintic_term
    ).astype(jnp.bfloat16)


def apply_fast(queries, updated):
    gate_pre = jnp.einsum(
        "thi,hij->thj", queries, updated[:, 0], preferred_element_type=jnp.float32
    )
    up_pre = jnp.einsum("thi,hij->thj", queries, updated[:, 1], preferred_element_type=jnp.float32)
    hidden = (jax.nn.silu(gate_pre) * up_pre).astype(jnp.bfloat16)
    output = jnp.einsum("thj,hij->thi", hidden, updated[:, 2], preferred_element_type=jnp.float32)
    return rms_rows(output, 1e-05).astype(jnp.bfloat16)


def shards(group_in, w_qkv, w_out, step_sizes, fast_weights, momentum, momentum_decay, fast_rate):
    tokens = group_in[0]
    tok_rows = tokens.shape[0]
    local_heads = fast_weights.shape[1]
    fan_width = fast_weights.shape[3]
    hid_width = fast_weights.shape[4]
    half_width = w_qkv.shape[3]
    projected = jnp.einsum(
        "td,jde->jte",
        tokens,
        lax.all_gather(w_qkv[0], "tok", axis=1, tiled=True),
        preferred_element_type=jnp.float32,
    )
    shaped = projected.reshape(3, tok_rows, local_heads, fan_width)
    queries = rms_rows(shaped[0], 1e-06).astype(jnp.bfloat16)
    key_rows = rms_rows(shaped[1], 1e-06).astype(jnp.bfloat16)
    value_rows = shaped[2].astype(jnp.bfloat16)
    gradients = fast_grads(key_rows, value_rows, step_sizes[0], fast_weights[0])
    decay_rate = momentum_decay[0][:, None, None, None]
    summed = lax.psum(gradients.astype(jnp.bfloat16), "tok").astype(jnp.float32)
    moment = decay_rate * momentum[0].astype(jnp.float32) + summed
    norm_values = jnp.sqrt(jnp.sum(moment * moment, axis=(2, 3), keepdims=True))
    iterate = (moment / (norm_values + 1e-06)).astype(jnp.bfloat16)
    iterate = iterate.reshape(local_heads * 3, fan_width, hid_width)
    for number in range(NS_ITERS):
        iterate = newton_step(iterate, iterate)
    iterate = iterate.reshape(local_heads, 3, fan_width, hid_width)
    updated = (
        fast_weights[0].astype(jnp.float32)
        - fast_rate[0][:, None, None, None] * iterate.astype(jnp.float32)
    ).astype(jnp.bfloat16)
    mixed_heads = apply_fast(queries, updated).reshape(tok_rows, half_width)
    partial_out = jnp.dot(
        mixed_heads,
        lax.all_gather(w_out[0], "tok", axis=1, tiled=True),
        preferred_element_type=jnp.float32,
    )
    summed_out = lax.psum_scatter(
        partial_out.astype(jnp.bfloat16), "head", scatter_dimension=1, tiled=True
    ).astype(jnp.float32)
    share_width = summed_out.shape[1]
    own_tokens = lax.dynamic_slice_in_dim(
        tokens, lax.axis_index("head") * share_width, share_width, 1
    )
    layer_out = (own_tokens.astype(jnp.float32) + summed_out).astype(jnp.bfloat16)
    handed = passed_along(layer_out[None], "section", 1)
    return (handed, updated[None])


def solution(mesh):
    placed = (
        P("section", "tok", None),
        P("section", None, "tok", "head"),
        P("section", "head", "tok"),
        P("section", "tok", "head"),
        P("section", "head", None, None, None),
        P("section", "head", None, None, None),
        P("section", "head"),
        P("section", "head"),
    )
    return jax.shard_map(
        shards,
        mesh=mesh,
        in_specs=placed,
        out_specs=(P("section", "tok", "head"), P("section", "head", None, None, None)),
        check_vma=False,
    )
```

profile of v0, /device:TPU:0, one launch (start us, length us, event | category | flops | bytes accessed | tf_op | source)
XLA Modules:
  0.0 475.3 jit_solution(7633743241635436623)
XLA Ops:
  7.2 4.6 copy.23
  11.9 1.8 copy-done.1
  13.7 1.8 copy.51
  15.6 217.4 %all-gather.5.cloned.1.call-done = bf16[1,3,2048,1024]{2,3,1,0:T(8,128)(2,1)} async-done(((bf16[1,3,512,1024]{2,3,1,0:T(8,128)(2,1)}), bf16[1,3,2048,1024]{2,3,1,0:T(8,128)(2,1)}) %all-gather.5.cloned.1.call-update) | async-done | bytes 12582928 | tf_op jit(solution)/shard_map/all_gather | solution.py:83
  232.9 6.6 %fusion.19 = f32[3,128,1024]{1,2,0:T(8,128)S(1)} fusion(bf16[1,3,2048,1024]{2,3,1,0:T(8,128)(2,1)} %all-gather.5.cloned.1.call-done, bf16[1,128,2048]{2,1,0:T(8,128)(2,1)} %param.8), kind=kOutput, calls=%fused_computation.27 | convolution fusion | flops 1610612736 | bytes 14680064 | tf_op jit(solution)/shard_map/td,jde->jte/dot_general | solution.py:80
  244.2 2.0 pad_maximum_fusion
  247.2 2.0 copy.31
  250.5 115.1 %all-reduce.2.cloned.1.call-done = bf16[2,3,512,512]{3,2,0,1:T(8,128)(2,1)} async-done(((bf16[2,3,512,512]{3,2,0,1:T(8,128)(2,1)}), bf16[2,3,512,512]{3,2,0,1:T(8,128)(2,1)}) %all-reduce.2.cloned.1.call-update) | async-done | bytes 3145744 | tf_op jit(solution)/shard_map/psum | solution.py:92
  365.6 3.5 multiply_reduce_fusion
  369.1 1.3 divide_convert_fusion
  370.6 1.8 convolution_convert_fusion.1
  372.5 1.8 fusion.48
  374.3 2.2 add_convert_fusion.1
  376.5 1.8 convolution_convert_fusion
  378.4 1.8 fusion.49
  380.2 2.5 fusion.7
  382.7 5.4 %fusion.4 = bf16[2,3,512,512]{3,2,0,1:T(8,128)(2,1)S(1)} fusion(f32[2,3,512,512]{3,2,1,0:T(8,128)S(1)} %bitcast.108, f32[2]{0:T(128)S(1)} %bitcast.120, bf16[1,2,3,512,512]{4,3,2,1,0:T(8,128)(2,1)} %param.12), kind=kLoop, calls=%fused_computation.6 | loop fusion | flops 6291456 | bytes 12582920 | tf_op jit(solution)/shard_map/convert_element_type | solution.py:103
  389.2 2.8 multiply_reduce_fusion.1
  393.1 53.9 %all-gather.7.cloned.1.call-done = bf16[1,1024,2048]{2,1,0:T(8,128)(2,1)} async-done(((bf16[1,1024,512]{2,1,0:T(8,128)(2,1)}), bf16[1,1024,2048]{2,1,0:T(8,128)(2,1)}) %all-gather.7.cloned.1.call-update) | async-done | bytes 4194320 | tf_op jit(solution)/shard_map/all_gather | solution.py:107
  447.0 3.9 fusion.16
  450.9 6.6 %reduce-scatter.2.cloned.1.call-done = bf16[128,1024]{1,0:T(8,128)(2,1)} async-done(((bf16[128,2048]{1,0:T(8,128)(2,1)}), bf16[128,1024]{1,0:T(8,128)(2,1)}) %reduce-scatter.2.cloned.1.call-update) | async-done | bytes 262160 | tf_op jit(solution)/shard_map/reduce_scatter | solution.py:110
  458.6 1.7 collective-permute-start
  460.3 5.6 %subtract_convert_fusion = bf16[1,2,3,512,512]{4,3,2,1,0:T(8,128)(2,1)} fusion(f32[1,2,3,512,512]{4,3,2,1,0:T(8,128)} %bitcast.109, bf16[1,2,3,512,512]{4,3,2,1,0:T(8,128)(2,1)S(1)} %copy-done.2, f32[2]{0:T(128)S(1)} %bitcast.121), kind=kLoop, calls=%fused_computation.7 | loop fusion | flops 6291456 | bytes 12582920 | tf_op jit(solution)/shard_map/convert_element_type | solution.py:103
  465.9 2.2 collective-permute-done
  (47 shorter events, 11.2 us)
Async XLA Ops:
  7.2 225.8 %all-gather.5.cloned.1.call-start = ((), (), s32[]{:S(2)}) async-start(), calls=%async_computation.3 | async-start | bytes 15728640 | tf_op jit(solution)/shard_map/all_gather | solution.py:83
  11.8 1.9 copy-start.1
  11.9 353.8 %all-reduce.2.cloned.1.call-start = ((), (), s32[]{:S(2)}) async-start(), calls=%async_computation.1 | async-start | bytes 6291456 | tf_op jit(solution)/shard_map/psum | solution.py:92
  239.5 2.1 copy-start.3
  240.4 1.9 copy-start.9
  246.2 119.4 %copy-start.4 = (bf16[1,2,3,512,512]{4,3,2,1,0:T(8,128)(2,1)S(1)}, bf16[1,2,3,512,512]{4,3,2,1,0:T(8,128)(2,1)}, u32[]{:S(2)}) copy-start(bf16[1,2,3,512,512]{4,3,2,1,0:T(8,128)(2,1)} %param.13) | copy-start | bytes 9437188
  246.2 119.4 %copy-start.8 = (f32[1,2]{1,0:T(1,128)S(1)}, f32[1,2]{1,0:T(1,128)}, u32[]{:S(2)}) copy-start(f32[1,2]{1,0:T(1,128)} %param.14) | copy-start | bytes 28
  246.2 200.7 %all-gather.7.cloned.1.call-start = ((), (), s32[]{:S(2)}) async-start(), calls=%async_computation.4 | async-start | bytes 5242880 | tf_op jit(solution)/shard_map/all_gather | solution.py:107
  247.0 210.5 %reduce-scatter.2.cloned.1.call-start = ((), (), s32[]{:S(2)}) async-start(), calls=%async_computation.2 | async-start | bytes 786432 | tf_op jit(solution)/shard_map/reduce_scatter | solution.py:110
  365.6 3.5 copy-start.5
  380.2 2.5 copy-start.7
  382.7 5.4 %copy-start = (f32[6,512,512]{2,1,0:T(8,128)}, f32[6,512,512]{2,1,0:T(8,128)S(1)}, u32[]{:S(2)}) copy-start(f32[6,512,512]{2,1,0:T(8,128)S(1)} %fusion.7) | copy-start | bytes 18874372
  382.7 5.4 %copy-start.6 = (f32[128,2,512]{2,0,1:T(8,128)S(1)}, f32[128,2,512]{2,0,1:T(8,128)}, u32[]{:S(2)}) copy-start(f32[128,2,512]{2,0,1:T(8,128)} %copy.31) | copy-start | bytes 1572868
  447.0 13.3 %copy-start.2 = (bf16[1,2,3,512,512]{4,3,2,1,0:T(8,128)(2,1)S(1)}, bf16[1,2,3,512,512]{4,3,2,1,0:T(8,128)(2,1)}, u32[]{:S(2)}) copy-start(bf16[1,2,3,512,512]{4,3,2,1,0:T(8,128)(2,1)} %param.12) | copy-start | bytes 9437188
  458.6 9.5 %collective-permute-start = (bf16[1,128,1024]{2,1,0:T(8,128)(2,1)S(1)}, bf16[1,128,1024]{2,1,0:T(8,128)(2,1)S(1)}, u32[]{:S(2)}, u32[]{:S(2)}) collective-permute-start(bf16[1,128,1024]{2,1,0:T(8,128)(2,1)S(1)} %fusion.36), channel_id=1, source_target_pairs={{0,8},{8,16},{16,24},{24,0},{1,9},{9,17},{17,25},{25,1},{2,10},{10... | collective-permute-start | bytes 786440 | tf_op jit(solution)/shard_map/ppermute | solution.py:15
Sparse Core Ops, SparseCore 0:
  12.0 220.8 all-gather.4
  246.4 119.2 all-reduce.1
  367.2 79.7 all-gather.6
  451.0 6.3 reduce-scatter.1
where the time goes:
time: 476 us; the launch traced here: 475 us
  waiting for transfers between devices  396 us (83%)
  matrix products  28.9 us (6%)
  other arithmetic  21.3 us (4%)
  between operations  14 us (3%)
  local copies, waits for them, and re-layouts  13.2 us (3%)
    all_gather x1, waiting for transfers between devices, shards(): lax.all_gather(w_qkv[0], 'tok', axis=1, tiled=True)  217 us
    psum x1, waiting for transfers between devices, shards(): summed = lax.psum(gradients.astype(jnp.bfloat16), 'tok').astype(jnp.float32)  115 us
    all_gather x1, waiting for transfers between devices, shards(): lax.all_gather(w_out[0], 'tok', axis=1, tiled=True)  53.9 us
    convert_element_type x2, other arithmetic, shards(): updated = (fast_weights[0].astype(jnp.float32) - fast_rate[0][:, None, No...  10.9 us
    unnamed x23, local copies, waits for them, and re-layouts  10.1 us
  transfers between devices with their start and end apart: 5, of which 5 were waited for; matrix products, arithmetic and copies ran while one was open for 8% of the time, Pallas kernels for 0%

commit v1 on v0

--- a/solution.py
+++ b/solution.py
@@ -2,11 +2,13 @@
 import jax.numpy as jnp
 from jax import lax
 from jax.sharding import PartitionSpec as P
+from jax.lax import all_gather
 
 NS_ITERS = 2
 coef_linear = 3.4445
 coef_cubic = -4.775
 coef_quintic = 2.0315
+_bind_vectors = lambda mine_x: jnp.concatenate(all_gather(mine_x, axis_name="tok"), axis=1)
 
 
 def passed_along(value, axis, steps):
@@ -102,11 +104,7 @@
         - fast_rate[0][:, None, None, None] * iterate.astype(jnp.float32)
     ).astype(jnp.bfloat16)
     mixed_heads = apply_fast(queries, updated).reshape(tok_rows, half_width)
-    partial_out = jnp.dot(
-        mixed_heads,
-        lax.all_gather(w_out[0], "tok", axis=1, tiled=True),
-        preferred_element_type=jnp.float32,
-    )
+    partial_out = jnp.dot(mixed_heads, _bind_vectors(w_out[0]), preferred_element_type=jnp.float32)
     summed_out = lax.psum_scatter(
         partial_out.astype(jnp.bfloat16), "head", scatter_dimension=1, tiled=True
     ).astype(jnp.float32)

time: 476 us -> 494 us (1.038)
  waiting for transfers between devices: 396 us -> 407 us
  local copies, waits for them, and re-layouts: 13.2 us -> 19.2 us
    all_gather x1, waiting for transfers between devices: 53.9 us -> 66.9 us  [all_gather(mine_x, axis_name='tok')]
    all_gather x0 -> x1, local copies, waits for them, and re-layouts: none -> 6.28 us  [all_gather(mine_x, axis_name='tok')]
  transfers between devices with their start and end apart: 5 -> 5, of which waited for: 5 -> 5; matrix products, arithmetic and copies ran while one was open for 8% -> 6% of each run, Pallas kernels for 0% -> 0%
where the time goes in v1:
time: 494 us; the launch traced here: 493 us
  waiting for transfers between devices  407 us (82%)
  matrix products  29.7 us (6%)
  other arithmetic  21.2 us (4%)
  local copies, waits for them, and re-layouts  19.2 us (4%)
  between operations  14 us (3%)
    all_gather x1, waiting for transfers between devices, shards(): lax.all_gather(w_qkv[0], 'tok', axis=1, tiled=True)  217 us
    psum x1, waiting for transfers between devices, shards(): summed = lax.psum(gradients.astype(jnp.bfloat16), 'tok').astype(jnp.float32)  113 us
    all_gather x1, waiting for transfers between devices, all_gather(mine_x, axis_name='tok')  66.9 us
    convert_element_type x2, other arithmetic, shards(): updated = (fast_weights[0].astype(jnp.float32) - fast_rate[0][:, None, No...  10.9 us
  transfers between devices with their start and end apart: 5, of which 5 were waited for; matrix products, arithmetic and copies ran while one was open for 6% of the time, Pallas kernels for 0%

profile of v1, /device:TPU:0, one launch (start us, length us, event | category | flops | bytes accessed | tf_op | source)
XLA Modules:
  0.0 493.1 jit_solution(15038829600062195262)
XLA Ops:
  7.2 4.6 copy.37
  13.7 1.8 copy.70
  15.6 217.4 %all-gather.6.cloned.1.call-done = bf16[1,3,2048,1024]{2,3,1,0:T(8,128)(2,1)} async-done(((bf16[1,3,512,1024]{2,3,1,0:T(8,128)(2,1)}), bf16[1,3,2048,1024]{2,3,1,0:T(8,128)(2,1)}) %all-gather.6.cloned.1.call-update) | async-done | bytes 12582928 | tf_op jit(solution)/shard_map/all_gather | solution.py:85
  232.9 6.6 %fusion.14 = f32[3,128,1024]{1,2,0:T(8,128)S(1)} fusion(bf16[1,3,2048,1024]{2,3,1,0:T(8,128)(2,1)} %all-gather.6.cloned.1.call-done, bf16[1,128,2048]{2,1,0:T(8,128)(2,1)} %param.8), kind=kOutput, calls=%fused_computation.25 | convolution fusion | flops 1610612736 | bytes 14680064 | tf_op jit(solution)/shard_map/td,jde->jte/dot_general | solution.py:82
  244.5 2.0 pad_maximum_fusion
  246.6 66.9 %all-gather.4.cloned.1.call-done = bf16[4,1024,512]{2,1,0:T(8,128)(2,1)} async-done(((bf16[1,1024,512]{2,1,0:T(8,128)(2,1)}), bf16[4,1024,512]{2,1,0:T(8,128)(2,1)}) %all-gather.4.cloned.1.call-update) | async-done | bytes 4194320 | tf_op jit(solution)/shard_map/all_gather | solution.py:11
  313.5 6.3 %copy.50 = bf16[4,1024,512]{1,2,0:T(8,128)(2,1)} copy(bf16[4,1024,512]{2,1,0:T(8,128)(2,1)} %all-gather.4.cloned.1.call-done) | data formatting | bytes 8388608 | tf_op jit(solution)/shard_map/all_gather | solution.py:11
  319.7 2.2 copy.45
  323.1 112.9 %all-reduce.2.cloned.1.call-done = bf16[2,3,512,512]{3,2,0,1:T(8,128)(2,1)} async-done(((bf16[2,3,512,512]{3,2,0,1:T(8,128)(2,1)}), bf16[2,3,512,512]{3,2,0,1:T(8,128)(2,1)}) %all-reduce.2.cloned.1.call-update) | async-done | bytes 3145744 | tf_op jit(solution)/shard_map/psum | solution.py:94
  436.0 3.5 multiply_reduce_fusion
  439.5 1.3 divide_convert_fusion
  441.0 1.8 convolution_convert_fusion.2
  442.8 1.8 fusion.43
  444.6 2.2 add_convert_fusion.1
  446.9 1.8 convolution_convert_fusion.1
  448.7 1.8 fusion.44
  450.5 2.5 fusion.5
  453.1 5.4 %fusion.4 = bf16[2,3,512,512]{3,2,0,1:T(8,128)(2,1)S(1)} fusion(f32[2,3,512,512]{3,2,1,0:T(8,128)S(1)} %bitcast.107, f32[2]{0:T(128)S(1)} %bitcast.120, bf16[1,2,3,512,512]{4,3,2,1,0:T(8,128)(2,1)} %param.12), kind=kLoop, calls=%fused_computation.6 | loop fusion | flops 6291456 | bytes 12582920 | tf_op jit(solution)/shard_map/convert_element_type | solution.py:105
  459.6 2.8 multiply_reduce_fusion.1
  463.5 4.7 convolution_convert_fusion
  468.2 7.1 %reduce-scatter.2.cloned.1.call-done = bf16[128,1024]{1,0:T(8,128)(2,1)} async-done(((bf16[128,2048]{1,0:T(8,128)(2,1)}), bf16[128,1024]{1,0:T(8,128)(2,1)}) %reduce-scatter.2.cloned.1.call-update) | async-done | bytes 262160 | tf_op jit(solution)/shard_map/reduce_scatter | solution.py:108
  476.4 1.7 collective-permute-start
  478.1 5.6 %subtract_convert_fusion = bf16[1,2,3,512,512]{4,3,2,1,0:T(8,128)(2,1)} fusion(f32[1,2,3,512,512]{4,3,2,1,0:T(8,128)} %bitcast.108, bf16[1,2,3,512,512]{4,3,2,1,0:T(8,128)(2,1)S(1)} %copy-done.2, f32[2]{0:T(128)S(1)} %bitcast.121), kind=kLoop, calls=%fused_computation.7 | loop fusion | flops 6291456 | bytes 12582920 | tf_op jit(solution)/shard_map/convert_element_type | solution.py:105
  483.7 2.2 collective-permute-done
  (48 shorter events, 12.3 us)
Async XLA Ops:
  7.2 225.8 %all-gather.6.cloned.1.call-start = ((), (), s32[]{:S(2)}) async-start(), calls=%async_computation.4 | async-start | bytes 15728640 | tf_op jit(solution)/shard_map/all_gather | solution.py:85
  11.8 1.9 copy-start.1
  11.9 301.6 %all-gather.4.cloned.1.call-start = ((), (), s32[]{:S(2)}) async-start(), calls=%async_computation.2 | async-start | bytes 5242880 | tf_op jit(solution)/shard_map/all_gather | solution.py:11
  12.6 423.4 %all-reduce.2.cloned.1.call-start = ((), (), s32[]{:S(2)}) async-start(), calls=%async_computation.1 | async-start | bytes 6291456 | tf_op jit(solution)/shard_map/psum | solution.py:94
  239.5 2.4 copy-start.3
  239.5 2.7 copy-start.9
  246.5 189.5 %copy-start.4 = (bf16[1,2,3,512,512]{4,3,2,1,0:T(8,128)(2,1)S(1)}, bf16[1,2,3,512,512]{4,3,2,1,0:T(8,128)(2,1)}, u32[]{:S(2)}) copy-start(bf16[1,2,3,512,512]{4,3,2,1,0:T(8,128)(2,1)} %param.13) | copy-start | bytes 9437188
  246.5 189.5 %copy-start.8 = (f32[1,2]{1,0:T(1,128)S(1)}, f32[1,2]{1,0:T(1,128)}, u32[]{:S(2)}) copy-start(f32[1,2]{1,0:T(1,128)} %param.14) | copy-start | bytes 28
  246.5 228.8 %reduce-scatter.2.cloned.1.call-start = ((), (), s32[]{:S(2)}) async-start(), calls=%async_computation.3 | async-start | bytes 786432 | tf_op jit(solution)/shard_map/reduce_scatter | solution.py:108
  436.0 3.5 copy-start.5
  450.5 2.5 copy-start.7
  453.0 5.4 %copy-start = (f32[6,512,512]{2,1,0:T(8,128)}, f32[6,512,512]{2,1,0:T(8,128)S(1)}, u32[]{:S(2)}) copy-start(f32[6,512,512]{2,1,0:T(8,128)S(1)} %fusion.5) | copy-start | bytes 18874372
  453.1 5.4 %copy-start.6 = (f32[128,2,512]{2,0,1:T(8,128)S(1)}, f32[128,2,512]{2,0,1:T(8,128)}, u32[]{:S(2)}) copy-start(f32[128,2,512]{2,0,1:T(8,128)} %copy.45) | copy-start | bytes 1572868
  463.5 14.6 %copy-start.2 = (bf16[1,2,3,512,512]{4,3,2,1,0:T(8,128)(2,1)S(1)}, bf16[1,2,3,512,512]{4,3,2,1,0:T(8,128)(2,1)}, u32[]{:S(2)}) copy-start(bf16[1,2,3,512,512]{4,3,2,1,0:T(8,128)(2,1)} %param.12) | copy-start | bytes 9437188
  476.4 9.4 %collective-permute-start = (bf16[1,128,1024]{2,1,0:T(8,128)(2,1)S(1)}, bf16[1,128,1024]{2,1,0:T(8,128)(2,1)S(1)}, u32[]{:S(2)}, u32[]{:S(2)}) collective-permute-start(bf16[1,128,1024]{2,1,0:T(8,128)(2,1)S(1)} %fusion.31), channel_id=1, source_target_pairs={{0,8},{8,16},{16,24},{24,0},{1,9},{9,17},{17,25},{25,1},{2,10},{10... | collective-permute-start | bytes 786440 | tf_op jit(solution)/shard_map/ppermute | solution.py:17
Sparse Core Ops, SparseCore 0:
  12.0 220.8 all-gather.5
  234.5 78.9 all-gather.3
  316.4 119.5 all-reduce.1
  468.3 6.9 reduce-scatter.1
